TPU v7x, 32 devices: a whole 2x2x4 slice. The times are simulated.
32 devices in a mesh: groups: 2 (over x), blk: 8 (over z, y), dp: 2 (over core).
Axes of the slice: x: 2, y: 2, z: 4, core: 2. Of those that a mesh axis runs over, the one named last changes fastest.
Arguments:
- particles: bfloat16 [32768, 4096], P(('groups', 'blk', 'dp')), parts along dimension 0, may hold values from -44 to 44
- defocus: int32 [32768], P(('groups', 'blk', 'dp')), parts along dimension 0, may hold values from 0 to 15
- pick_dest: int32 [32768, 1], P(('groups', 'blk', 'dp')), parts along dimension 0, may hold values from 0 to 15; in each aligned block of 1024 rows (0 to 1023, 1024 to 2047, ...) at most 128 rows name the same one
- references: bfloat16 [192, 4096], P(('groups', 'blk')), parts along dimension 0, may hold values from -4 to 4
- ctf_table: float32 [32, 4096], P('groups'), parts along dimension 0, may hold values from 0.1 to 1
Outputs:
- weighted_sums: float32 [192, 4096], P(('groups', 'blk', 'dp')), parts along dimension 0
- ctf_weights: float32 [192, 4096], P(('groups', 'blk', 'dp')), parts along dimension 0
- posterior: float32 [65536, 96], P(('groups', 'blk', 'dp')), parts along dimension 0
There are 2 independent parts, one for each index of `groups`. A program takes and returns all parts, laid end to end along the dimension named above; each array names one. Nothing has to cross between parts.
Inputs may be any that keep to these rules, and one draw needn't show every extreme that they name: `pick_dest`: of the particles that one device holds, at most 128 name any one destination, and in every draw some device sends exactly 128 to one destination.
All inputs are finite; a program needn't handle non-finite values.
Results may differ from a plain program's by a relative error of at most 0.0028.
Values may be sent and summed in bfloat16 or wider, within the bound.
A program may use at most 128 MiB of HBM per device.

v0:
```python
import math
import jax
import jax.numpy as jnp
from jax import lax
from jax.sharding import PartitionSpec as P

PIX = 4096


def lookup(class_ids, table_rows):
    return (class_ids[:, None] == jnp.arange(table_rows, dtype=jnp.int32)[None, :]).astype(
        jnp.float32
    )


def per_device(particles, defocus, pick_dest, references, ctf_table):
    held_rows = particles.shape[0]
    table_rows = ctf_table.shape[0]
    kr_total = references.shape[0] * lax.axis_size("blk")
    device_count = lax.axis_size(("blk", "dp"))
    capacity = max(2, 2 * held_rows // device_count)
    recv_rows = device_count * capacity
    rows_mine = kr_total // device_count
    score_scale = 1.0 / math.sqrt(PIX)
    ctf_square = ctf_table * ctf_table
    own_onehot = lookup(defocus, table_rows)
    modulation = jnp.dot(own_onehot, ctf_table, precision=lax.Precision.HIGHEST)
    modulated = (particles.astype(jnp.float32) * modulation).astype(jnp.bfloat16)
    destination = pick_dest[:, 0]
    dest_hot = (destination[:, None] == jnp.arange(device_count, dtype=jnp.int32)[None, :]).astype(
        jnp.int32
    )
    earlier = jnp.cumsum(dest_hot, axis=0) - dest_hot
    ranking = jnp.sum(earlier * dest_hot, axis=1)
    slot_index = destination * capacity + ranking
    ref_piece = lax.all_gather(references, "blk", axis=0, tiled=True)
    cross_term = lax.dot_general(
        modulated, ref_piece, (((1,), (1,)), ((), ())), preferred_element_type=jnp.float32
    )
    piece_float = ref_piece.astype(jnp.float32)
    quadratic = 0.5 * lax.dot_general(
        ctf_square,
        piece_float * piece_float,
        (((1,), (1,)), ((), ())),
        precision=lax.Precision.HIGHEST,
    )
    scores = score_scale * (
        cross_term - jnp.dot(own_onehot, quadratic, precision=lax.Precision.HIGHEST)
    )
    largest = jnp.max(scores, axis=1, keepdims=True)
    exponent = jnp.exp(scores - largest)
    weights = exponent / jnp.sum(exponent, axis=1, keepdims=True)
    send_weights = jnp.zeros((recv_rows, kr_total), jnp.float32).at[slot_index].set(weights)
    posterior = lax.all_to_all(send_weights, ("blk", "dp"), split_axis=0, concat_axis=0, tiled=True)
    weights_low = weights.astype(jnp.bfloat16)
    weighted_sums = lax.psum_scatter(
        lax.dot_general(
            weights_low, modulated, (((0,), (0,)), ((), ())), preferred_element_type=jnp.float32
        ),
        ("blk", "dp"),
        scatter_dimension=0,
        tiled=True,
    )
    class_sums = lax.dot_general(
        own_onehot, weights, (((0,), (0,)), ((), ())), precision=lax.Precision.HIGHEST
    )
    totals = lax.psum(class_sums, ("blk", "dp"))
    own_sums = lax.dynamic_slice_in_dim(
        totals, lax.axis_index(("blk", "dp")) * rows_mine, rows_mine, 1
    )
    ctf_weights = lax.dot_general(
        own_sums, ctf_square, (((0,), (0,)), ((), ())), precision=lax.Precision.HIGHEST
    )
    return (weighted_sums, ctf_weights, posterior)


def solution(mesh):
    placed = (
        P(("groups", "blk", "dp"), None),
        P(("groups", "blk", "dp")),
        P(("groups", "blk", "dp"), None),
        P(("groups", "blk"), None),
        P("groups", None),
    )
    return jax.shard_map(
        per_device,
        mesh=mesh,
        in_specs=placed,
        out_specs=(
            P(("groups", "blk", "dp"), None),
            P(("groups", "blk", "dp"), None),
            P(("groups", "blk", "dp"), None),
        ),
        check_vma=False,
    )
```

profile of v0, /device:TPU:0, one launch (start us, length us, event | category | flops | bytes accessed | tf_op | source)
XLA Modules:
  0.0 189.7 jit_solution(3554859009608589075)
XLA Ops:
  0.6 34.8 %all-gather = bf16[8,12,4096]{2,1,0:T(8,128)(2,1)S(1)} all-gather(bf16[1,12,4096]{2,1,0:T(8,128)(2,1)} %bitcast.40), channel_id=1, replica_groups=mesh['groups'=2,'blk'=8,'dp'=2] {'blk'}, dimensions={0}, use_global_device_ids=true | all-gather | bytes 884736 | tf_op jit(solution)/shard_map/all_gather | solution.py:36
  35.4 0.2 reshape.38
  35.6 2.3 %fusion.5 = f32[16,96]{1,0:T(8,128)S(1)} fusion(bf16[96,4096]{1,0:T(8,128)(2,1)S(1)} %reshape.38, f32[16,4096]{1,0:T(8,128)} %param.9), kind=kOutput, calls=%fused_computation.7 | convolution fusion | flops 76350976 | bytes 1054720 | tf_op jit(solution)/shard_map/dot_general | solution.py:41
  37.9 9.8 %multiply_convert_fusion = bf16[1024,4096]{1,0:T(8,128)(2,1)S(1)} fusion(bf16[1024,4096]{1,0:T(8,128)(2,1)} %param.5, f32[16,4096]{1,0:T(8,128)} %param.9, s32[1024]{0:T(1024)} %param.6), kind=kOutput, calls=%fused_computation.1 | convolution fusion | flops 817905664 | bytes 17043456 | tf_op jit(solution)/shard_map/dot_general | solution.py:27
  47.7 0.0 copy-start
  47.7 3.2 %copy-done = bf16[1024,4096]{1,0:T(8,128)(2,1)} copy-done((bf16[1024,4096]{1,0:T(8,128)(2,1)}, bf16[1024,4096]{1,0:T(8,128)(2,1)S(1)}, u32[]{:S(2)}) %copy-start) | copy-done | bytes 8388632
  51.0 0.0 copy-start.2
  51.0 0.0 copy-start.3
  51.0 2.7 %fusion.28 = f32[1024,96]{0,1:T(8,128)S(1)} fusion(bf16[1024,4096]{1,0:T(8,128)(2,1)S(1)} %multiply_convert_fusion, bf16[96,4096]{1,0:T(8,128)(2,1)S(1)} %reshape.38), kind=kOutput, calls=%fused_computation.37 | convolution fusion | flops 805306368 | bytes 9568256 | tf_op jit(solution)/shard_map/dot_general | solution.py:37
  53.7 0.0 copy-done.2
  53.7 0.6 fusion.27
  54.3 0.1 fusion.12
  54.3 0.1 fusion.11
  54.4 0.2 copy.20
  54.6 0.0 copy-done.3
  54.6 4.5 %reduce-window.6 = s32[16,8,128]{2,1,0:T(8,128)S(1)} reduce-window(s32[16,8,128]{2,1,0:T(8,128)S(1)} %fusion.24, s32[]{:T(128)} %constant.6.clone.1), window={size=1x1x128 pad=0_0x0_0x127_0}, to_apply=%region_4.5 | reduce-window | flops 2080768 | bytes 131076 | tf_op jit(solution)/shard_map/reduce-window
  59.2 0.1 slice.8
  59.2 0.1 copy.18
  59.4 0.1 copy.19
  59.5 0.1 broadcast_add_fusion
  59.6 3.3 %scatter_custom_fusion = f32[2048,96]{1,0:T(8,128)S(1)} fusion(s32[1024]{0:T(1024)S(1)} %bitcast.45, f32[1024,96]{1,0:T(8,128)S(1)} %copy.20, f32[]{:T(128)} %constant.15.clone.1), kind=kCustom, calls=%fused_computation.9 | custom fusion | bytes 786436 | tf_op jit(solution)/shard_map/scatter | solution.py:53
  63.0 1.2 copy.21
  64.2 5.5 %all-to-all-start = ((f32[16,128,96]{1,2,0:T(8,128)}), f32[16,128,96]{1,2,0:T(8,128)S(1)}, u32[]{:S(2)}, u32[]{:S(2)}) async-start(f32[16,128,96]{1,2,0:T(8,128)} %copy.21), calls=%async_computation | async-start | bytes 1572864 | tf_op jit(solution)/shard_map/all_to_all | solution.py:54
  69.7 0.0 copy-start.1
  69.7 0.0 copy-start.4
  69.7 4.9 %fusion.19 = f32[96,4096]{1,0:T(8,128)S(1)} fusion(bf16[1024,4096]{1,0:T(8,128)(2,1)} %copy-done, f32[1024,96]{0,1:T(8,128)S(1)} %fusion.11), kind=kOutput, calls=%fused_computation.22 | convolution fusion | flops 805404672 | bytes 10354688 | tf_op jit(solution)/shard_map/dot_general | solution.py:57
  74.6 43.0 %fusion = f32[8,4096]{1,0:T(8,128)S(1)} fusion(f32[96,4096]{1,0:T(8,128)S(1)} %fusion.19), kind=kCustom, calls=%all-reduce-scatter | all-reduce-scatter fusion | flops 524289 | bytes 1704448
  117.6 1.3 collective-permute-start
  118.9 1.3 collective-permute-start.1
  120.2 2.2 %collective-permute-start.2 = (f32[8,4096]{1,0:T(8,128)S(1)}, f32[8,4096]{1,0:T(8,128)S(1)}, u32[]{:S(2)}, u32[]{:S(2)}) collective-permute-start(f32[8,4096]{1,0:T(8,128)S(1)} %fusion), channel_id=1, source_target_pairs={{0,3},{1,4},{2,5},{3,6},{4,7},{5,8},{6,9},{7,10},{8,11},{9,12},{10... | collective-permute-start | bytes 393224
  122.4 4.5 %collective-permute-start.3 = (f32[6,4096]{1,0:T(8,128)S(1)}, f32[6,4096]{1,0:T(8,128)S(1)}, u32[]{:S(2)}, u32[]{:S(2)}) collective-permute-start(f32[6,4096]{1,0:T(8,128)S(1)} %slice.10), channel_id=1, source_target_pairs={{0,4},{1,5},{2,6},{3,7},{4,8},{5,9},{6,10},{7,11},{8,12},{9,13},{1... | collective-permute-start | bytes 294920
  126.9 0.5 fusion.10
  127.4 57.7 %psum.7 = f32[16,96]{0,1:T(8,128)S(1)} all-reduce(f32[16,96]{0,1:T(8,128)S(1)} %fusion.10), channel_id=1, replica_groups=mesh['groups'=2,'blk'=8,'dp'=2] {'blk','dp'}, use_global_device_ids=true, to_apply=%region_3.4 | all-reduce | flops 1536 | bytes 12288 | tf_op jit(solution)/shard_map/psum | solution.py:67
  185.1 0.0 copy-done.1
  185.1 0.9 fusion.16
  186.0 0.0 copy-done.4
  186.0 0.6 dynamic-slice.4
  187.3 0.0 collective-permute-done.3
  187.3 0.0 collective-permute-done
  187.3 0.0 collective-permute-done.1
  187.3 0.0 collective-permute-done.2
  187.3 0.8 concatenate
  188.1 0.7 constant_dynamic-slice_fusion
  188.8 0.0 all-to-all-done
  188.8 0.9 copy_bitcast_fusion
  (6 shorter events, 0.1 us)
Async XLA Ops:
  47.7 3.2 %copy-start = (bf16[1024,4096]{1,0:T(8,128)(2,1)}, bf16[1024,4096]{1,0:T(8,128)(2,1)S(1)}, u32[]{:S(2)}) copy-start(bf16[1024,4096]{1,0:T(8,128)(2,1)S(1)} %multiply_convert_fusion) | copy-start | bytes 25165828
  51.0 2.7 %copy-start.2 = (s32[1024]{0:T(1024)S(1)}, s32[1024]{0:T(1024)}, u32[]{:S(2)}) copy-start(s32[1024]{0:T(1024)} %param.6) | copy-start | bytes 12292
  51.0 3.7 %copy-start.3 = (s32[1024,1]{0,1:T(1,128)S(1)}, s32[1024,1]{0,1:T(1,128)}, u32[]{:S(2)}) copy-start(s32[1024,1]{0,1:T(1,128)} %param.7) | copy-start | bytes 12292
  64.2 124.6 %all-to-all-start = ((f32[16,128,96]{1,2,0:T(8,128)}), f32[16,128,96]{1,2,0:T(8,128)S(1)}, u32[]{:S(2)}, u32[]{:S(2)}) async-start(f32[16,128,96]{1,2,0:T(8,128)} %copy.21), calls=%async_computation | async-start | bytes 1572864 | tf_op jit(solution)/shard_map/all_to_all | solution.py:54
  69.7 115.4 %copy-start.1 = (f32[16,4096]{1,0:T(8,128)S(1)}, f32[16,4096]{1,0:T(8,128)}, u32[]{:S(2)}) copy-start(f32[16,4096]{1,0:T(8,128)} %param.9) | copy-start | bytes 786436
  69.7 116.3 %copy-start.4 = (u32[32]{0:T(128)S(1)}, u32[32]{0:T(128)}, u32[]{:S(2)}) copy-start(u32[32]{0:T(128)} %constant.37) | copy-start | bytes 388
  117.6 69.7 %collective-permute-start = (f32[8,4096]{1,0:T(8,128)S(1)}, f32[8,4096]{1,0:T(8,128)S(1)}, u32[]{:S(2)}, u32[]{:S(2)}) collective-permute-start(f32[8,4096]{1,0:T(8,128)S(1)} %fusion), channel_id=1, source_target_pairs={{0,1},{1,2},{2,3},{3,4},{4,5},{5,6},{6,7},{7,8},{8,9},{9,10},{10,1... | collective-permute-start | bytes 393224
  118.9 68.4 %collective-permute-start.1 = (f32[8,4096]{1,0:T(8,128)S(1)}, f32[8,4096]{1,0:T(8,128)S(1)}, u32[]{:S(2)}, u32[]{:S(2)}) collective-permute-start(f32[8,4096]{1,0:T(8,128)S(1)} %fusion), channel_id=1, source_target_pairs={{0,2},{1,3},{2,4},{3,5},{4,6},{5,7},{6,8},{7,9},{8,10},{9,11},{10,... | collective-permute-start | bytes 393224
  120.2 67.1 %collective-permute-start.2 = (f32[8,4096]{1,0:T(8,128)S(1)}, f32[8,4096]{1,0:T(8,128)S(1)}, u32[]{:S(2)}, u32[]{:S(2)}) collective-permute-start(f32[8,4096]{1,0:T(8,128)S(1)} %fusion), channel_id=1, source_target_pairs={{0,3},{1,4},{2,5},{3,6},{4,7},{5,8},{6,9},{7,10},{8,11},{9,12},{10... | collective-permute-start | bytes 393224
  122.4 64.9 %collective-permute-start.3 = (f32[6,4096]{1,0:T(8,128)S(1)}, f32[6,4096]{1,0:T(8,128)S(1)}, u32[]{:S(2)}, u32[]{:S(2)}) collective-permute-start(f32[6,4096]{1,0:T(8,128)S(1)} %slice.10), channel_id=1, source_target_pairs={{0,4},{1,5},{2,6},{3,7},{4,8},{5,9},{6,10},{7,11},{8,12},{9,13},{1... | collective-permute-start | bytes 294920
where the time goes:
time: 190 us
  blocking collectives  136 us (72%)
  matrix products  21.6 us (11%)
  starting transfers between devices  14.8 us (8%)
  local copies, waits for them, and re-layouts  11.5 us (6%)
  other arithmetic  4.82 us (3%)
    psum x1, blocking collectives, per_device(): totals = lax.psum(class_sums, ('blk', 'dp'))  57.7 us
    unnamed x1, blocking collectives  43 us
    all_gather x1, blocking collectives, per_device(): ref_piece = lax.all_gather(references, 'blk', axis=0, tiled=True)  34.8 us
    dot_general x1, matrix products, per_device(): modulation = jnp.dot(own_onehot, ctf_table, precision=lax.Precision.HIGHEST)  9.82 us
    unnamed x4, starting transfers between devices  9.27 us
    all_to_all x1, starting transfers between devices, per_device(): lax.all_to_all(send_weights, ('blk', 'dp'), split_axis=0, concat_axis=0,...  5.49 us
    unnamed x15, local copies, waits for them, and re-layouts  5.48 us
    dot_general x1, matrix products, per_device(): lax.dot_general(weights_low, modulated, (((0,), (0,)), ((), ())), preferr...  4.87 us
  transfers between devices with their start and end apart: 5, of which 0 were waited for; matrix products, arithmetic and copies ran while one was open for 27% of the time, Pallas kernels for 0%

commit v1 on v0

--- a/solution.py
+++ b/solution.py
@@ -64,7 +64,7 @@
     class_sums = lax.dot_general(
         own_onehot, weights, (((0,), (0,)), ((), ())), precision=lax.Precision.HIGHEST
     )
-    totals = lax.psum(class_sums, ("blk", "dp"))
+    totals = jnp.sum(jax.lax.all_gather(class_sums, ("blk", "dp")), axis=0)
     own_sums = lax.dynamic_slice_in_dim(
         totals, lax.axis_index(("blk", "dp")) * rows_mine, rows_mine, 1
     )

time: 190 us -> 150 us (0.79)
  blocking collectives: 136 us -> 95.5 us
    psum x1 -> x0, blocking collectives: 57.7 us -> none  [per_device(): totals = lax.psum(class_sums, ('blk', 'dp'))]
    all_gather x0 -> x1, blocking collectives: none -> 17.7 us  [per_device(): totals = jnp.sum(jax.lax.all_gather(class_sums, ('blk', 'dp')), axis=0)]
  transfers between devices with their start and end apart: 5 -> 5, of which waited for: 0 -> 0; matrix products, arithmetic and copies ran while one was open for 27% -> 34% of each run, Pallas kernels for 0% -> 0%
where the time goes in v1:
time: 150 us
  blocking collectives  95.5 us (64%)
  matrix products  21.9 us (15%)
  starting transfers between devices  14.8 us (10%)
  local copies, waits for them, and re-layouts  11.5 us (8%)
  other arithmetic  4.85 us (3%)
  between operations  1.53 us (1%)
    unnamed x1, blocking collectives  43 us
    all_gather x1, blocking collectives, per_device(): ref_piece = lax.all_gather(references, 'blk', axis=0, tiled=True)  34.8 us
    all_gather x1, blocking collectives, per_device(): totals = jnp.sum(jax.lax.all_gather(class_sums, ('blk', 'dp')), axis=0)  17.7 us
    dot_general x1, matrix products, per_device(): modulation = jnp.dot(own_onehot, ctf_table, precision=lax.Precision.HIGHEST)  9.82 us
    unnamed x4, starting transfers between devices  9.27 us
    all_to_all x1, starting transfers between devices, per_device(): lax.all_to_all(send_weights, ('blk', 'dp'), split_axis=0, concat_axis=0,...  5.49 us
    unnamed x15, local copies, waits for them, and re-layouts  5.48 us
    dot_general x1, matrix products, per_device(): lax.dot_general(weights_low, modulated, (((0,), (0,)), ((), ())), preferr...  4.87 us
  transfers between devices with their start and end apart: 5, of which 0 were waited for; matrix products, arithmetic and copies ran while one was open for 34% of the time, Pallas kernels for 0%

profile of v1, /device:TPU:0, one launch (start us, length us, event | category | flops | bytes accessed | tf_op | source)
XLA Modules:
  0.0 150.0 jit_solution(15171070898131193876)
XLA Ops:
  0.6 34.8 %all-gather.1 = bf16[8,12,4096]{2,1,0:T(8,128)(2,1)S(1)} all-gather(bf16[1,12,4096]{2,1,0:T(8,128)(2,1)} %bitcast.42), channel_id=1, replica_groups=mesh['groups'=2,'blk'=8,'dp'=2] {'blk'}, dimensions={0}, use_global_device_ids=true | all-gather | bytes 884736 | tf_op jit(solution)/shard_map/all_gather | solution.py:36
  35.4 0.2 reshape.39
  35.6 2.3 %fusion.5 = f32[16,96]{1,0:T(8,128)S(1)} fusion(bf16[96,4096]{1,0:T(8,128)(2,1)S(1)} %reshape.39, f32[16,4096]{1,0:T(8,128)} %param.9), kind=kOutput, calls=%fused_computation.7 | convolution fusion | flops 76350976 | bytes 1054720 | tf_op jit(solution)/shard_map/dot_general | solution.py:41
  37.9 9.8 %multiply_convert_fusion = bf16[1024,4096]{1,0:T(8,128)(2,1)S(1)} fusion(bf16[1024,4096]{1,0:T(8,128)(2,1)} %param.5, f32[16,4096]{1,0:T(8,128)} %param.9, s32[1024]{0:T(1024)} %param.6), kind=kOutput, calls=%fused_computation.1 | convolution fusion | flops 817905664 | bytes 17043456 | tf_op jit(solution)/shard_map/dot_general | solution.py:27
  47.7 0.0 copy-start
  47.7 3.2 %copy-done = bf16[1024,4096]{1,0:T(8,128)(2,1)} copy-done((bf16[1024,4096]{1,0:T(8,128)(2,1)}, bf16[1024,4096]{1,0:T(8,128)(2,1)S(1)}, u32[]{:S(2)}) %copy-start) | copy-done | bytes 8388632
  51.0 0.0 copy-start.2
  51.0 0.0 copy-start.3
  51.0 2.7 %fusion.30 = f32[1024,96]{0,1:T(8,128)S(1)} fusion(bf16[1024,4096]{1,0:T(8,128)(2,1)S(1)} %multiply_convert_fusion, bf16[96,4096]{1,0:T(8,128)(2,1)S(1)} %reshape.39), kind=kOutput, calls=%fused_computation.38 | convolution fusion | flops 805306368 | bytes 9568256 | tf_op jit(solution)/shard_map/dot_general | solution.py:37
  53.7 0.0 copy-done.2
  53.7 0.6 fusion.29
  54.3 0.1 fusion.12
  54.3 0.1 fusion.11
  54.4 0.2 copy.20
  54.6 0.0 copy-done.3
  54.6 4.5 %reduce-window.6 = s32[16,8,128]{2,1,0:T(8,128)S(1)} reduce-window(s32[16,8,128]{2,1,0:T(8,128)S(1)} %fusion.26, s32[]{:T(128)} %constant.6.clone.1), window={size=1x1x128 pad=0_0x0_0x127_0}, to_apply=%region_4.5 | reduce-window | flops 2080768 | bytes 131076 | tf_op jit(solution)/shard_map/reduce-window
  59.2 0.1 slice.8
  59.2 0.1 copy.18
  59.4 0.1 copy.19
  59.5 0.1 broadcast_add_fusion
  59.6 3.3 %scatter_custom_fusion = f32[2048,96]{1,0:T(8,128)S(1)} fusion(s32[1024]{0:T(1024)S(1)} %bitcast.47, f32[1024,96]{1,0:T(8,128)S(1)} %copy.20, f32[]{:T(128)} %constant.15.clone.1), kind=kCustom, calls=%fused_computation.9 | custom fusion | bytes 786436 | tf_op jit(solution)/shard_map/scatter | solution.py:53
  63.0 1.2 copy.21
  64.2 5.5 %all-to-all-start = ((f32[16,128,96]{1,2,0:T(8,128)}), f32[16,128,96]{1,2,0:T(8,128)S(1)}, u32[]{:S(2)}, u32[]{:S(2)}) async-start(f32[16,128,96]{1,2,0:T(8,128)} %copy.21), calls=%async_computation | async-start | bytes 1572864 | tf_op jit(solution)/shard_map/all_to_all | solution.py:54
  69.7 0.0 copy-start.1
  69.7 0.0 copy-start.4
  69.7 4.9 %fusion.21 = f32[96,4096]{1,0:T(8,128)S(1)} fusion(bf16[1024,4096]{1,0:T(8,128)(2,1)} %copy-done, f32[1024,96]{0,1:T(8,128)S(1)} %fusion.11), kind=kOutput, calls=%fused_computation.23 | convolution fusion | flops 805404672 | bytes 10354688 | tf_op jit(solution)/shard_map/dot_general | solution.py:57
  74.6 43.0 %fusion = f32[8,4096]{1,0:T(8,128)S(1)} fusion(f32[96,4096]{1,0:T(8,128)S(1)} %fusion.21), kind=kCustom, calls=%all-reduce-scatter | all-reduce-scatter fusion | flops 524289 | bytes 1704448
  117.6 1.3 collective-permute-start
  118.9 1.3 collective-permute-start.1
  120.2 2.2 %collective-permute-start.2 = (f32[8,4096]{1,0:T(8,128)S(1)}, f32[8,4096]{1,0:T(8,128)S(1)}, u32[]{:S(2)}, u32[]{:S(2)}) collective-permute-start(f32[8,4096]{1,0:T(8,128)S(1)} %fusion), channel_id=1, source_target_pairs={{0,3},{1,4},{2,5},{3,6},{4,7},{5,8},{6,9},{7,10},{8,11},{9,12},{10... | collective-permute-start | bytes 393224
  122.4 4.5 %collective-permute-start.3 = (f32[6,4096]{1,0:T(8,128)S(1)}, f32[6,4096]{1,0:T(8,128)S(1)}, u32[]{:S(2)}, u32[]{:S(2)}) collective-permute-start(f32[6,4096]{1,0:T(8,128)S(1)} %slice.10), channel_id=1, source_target_pairs={{0,4},{1,5},{2,6},{3,7},{4,8},{5,9},{6,10},{7,11},{8,12},{9,13},{1... | collective-permute-start | bytes 294920
  126.9 0.6 fusion.13
  127.5 17.7 %all-gather = f32[256,96]{1,0:T(8,128)S(1)} all-gather(f32[16,96]{1,0:T(8,128)S(1)} %fusion.13), channel_id=2, replica_groups=mesh['groups'=2,'blk'=8,'dp'=2] {'blk','dp'}, dimensions={0}, use_global_device_ids=true | all-gather | bytes 104448 | tf_op jit(solution)/shard_map/all_gather | solution.py:67
  145.3 0.0 copy-done.1
  145.3 1.0 fusion.18
  146.3 0.0 copy-done.4
  146.3 0.6 dynamic-slice.4
  147.6 0.0 collective-permute-done.3
  147.6 0.0 collective-permute-done
  147.6 0.0 collective-permute-done.1
  147.6 0.0 collective-permute-done.2
  147.6 0.8 concatenate
  148.4 0.7 constant_dynamic-slice_fusion
  149.1 0.0 all-to-all-done
  149.1 0.9 copy_bitcast_fusion
  (7 shorter events, 0.1 us)
Async XLA Ops:
  47.7 3.2 %copy-start = (bf16[1024,4096]{1,0:T(8,128)(2,1)}, bf16[1024,4096]{1,0:T(8,128)(2,1)S(1)}, u32[]{:S(2)}) copy-start(bf16[1024,4096]{1,0:T(8,128)(2,1)S(1)} %multiply_convert_fusion) | copy-start | bytes 25165828
  51.0 2.7 %copy-start.2 = (s32[1024]{0:T(1024)S(1)}, s32[1024]{0:T(1024)}, u32[]{:S(2)}) copy-start(s32[1024]{0:T(1024)} %param.6) | copy-start | bytes 12292
  51.0 3.7 %copy-start.3 = (s32[1024,1]{0,1:T(1,128)S(1)}, s32[1024,1]{0,1:T(1,128)}, u32[]{:S(2)}) copy-start(s32[1024,1]{0,1:T(1,128)} %param.7) | copy-start | bytes 12292
  64.2 84.9 %all-to-all-start = ((f32[16,128,96]{1,2,0:T(8,128)}), f32[16,128,96]{1,2,0:T(8,128)S(1)}, u32[]{:S(2)}, u32[]{:S(2)}) async-start(f32[16,128,96]{1,2,0:T(8,128)} %copy.21), calls=%async_computation | async-start | bytes 1572864 | tf_op jit(solution)/shard_map/all_to_all | solution.py:54
  69.7 75.6 %copy-start.1 = (f32[16,4096]{1,0:T(8,128)S(1)}, f32[16,4096]{1,0:T(8,128)}, u32[]{:S(2)}) copy-start(f32[16,4096]{1,0:T(8,128)} %param.9) | copy-start | bytes 786436
  69.7 76.6 %copy-start.4 = (u32[32]{0:T(128)S(1)}, u32[32]{0:T(128)}, u32[]{:S(2)}) copy-start(u32[32]{0:T(128)} %constant.37) | copy-start | bytes 388
  117.6 30.0 %collective-permute-start = (f32[8,4096]{1,0:T(8,128)S(1)}, f32[8,4096]{1,0:T(8,128)S(1)}, u32[]{:S(2)}, u32[]{:S(2)}) collective-permute-start(f32[8,4096]{1,0:T(8,128)S(1)} %fusion), channel_id=1, source_target_pairs={{0,1},{1,2},{2,3},{3,4},{4,5},{5,6},{6,7},{7,8},{8,9},{9,10},{10,1... | collective-permute-start | bytes 393224
  118.9 28.7 %collective-permute-start.1 = (f32[8,4096]{1,0:T(8,128)S(1)}, f32[8,4096]{1,0:T(8,128)S(1)}, u32[]{:S(2)}, u32[]{:S(2)}) collective-permute-start(f32[8,4096]{1,0:T(8,128)S(1)} %fusion), channel_id=1, source_target_pairs={{0,2},{1,3},{2,4},{3,5},{4,6},{5,7},{6,8},{7,9},{8,10},{9,11},{10,... | collective-permute-start | bytes 393224
  120.2 27.4 %collective-permute-start.2 = (f32[8,4096]{1,0:T(8,128)S(1)}, f32[8,4096]{1,0:T(8,128)S(1)}, u32[]{:S(2)}, u32[]{:S(2)}) collective-permute-start(f32[8,4096]{1,0:T(8,128)S(1)} %fusion), channel_id=1, source_target_pairs={{0,3},{1,4},{2,5},{3,6},{4,7},{5,8},{6,9},{7,10},{8,11},{9,12},{10... | collective-permute-start | bytes 393224
  122.4 25.1 %collective-permute-start.3 = (f32[6,4096]{1,0:T(8,128)S(1)}, f32[6,4096]{1,0:T(8,128)S(1)}, u32[]{:S(2)}, u32[]{:S(2)}) collective-permute-start(f32[6,4096]{1,0:T(8,128)S(1)} %slice.10), channel_id=1, source_target_pairs={{0,4},{1,5},{2,6},{3,7},{4,8},{5,9},{6,10},{7,11},{8,12},{9,13},{1... | collective-permute-start | bytes 294920
